TPU v7x, 512 devices: a whole 4x8x8 slice. The times are simulated.
512 devices in a mesh: scen: 32 (over z_hi, y, core), clus: 16 (over z_lo, x).
Axes of the slice: x: 4, y: 8, z: 8 (z_hi: 2, z_lo: 4; z = z_hi * 4 + z_lo), core: 2. Of those that a mesh axis runs over, the one named last changes fastest.
Arguments:
- factors: bfloat16 [512, 64, 36864], P('scen', 'clus'), may hold values from -0.4375 to 0.4375
- linear: float32 [512, 64, 192], P('scen', 'clus'), may hold values from -6 to 6
- arrival: int32 [512, 64], P('scen', 'clus'), may hold values from 0 to 47
- departure: int32 [512, 64], P('scen', 'clus'), may hold values from 48 to 96
- ev_count: int32 [64], P('clus'), may hold values from 8 to 48
- prob: float32 [512], P('scen'), may hold values from 0.5 to 13.5, as said below
- branch_of: int32 [512], P('scen'), may hold values from 0 to 7, as said below
- multiplier: float32 [512, 96], P('scen'), may hold values from -0.12 to 0.12
- root_prev: float32 [32], replicated, may hold values from -12 to 12
- branch_prev: float32 [8, 64], replicated, may hold values from -12 to 12
Outputs:
- power: float32 [512, 64, 192], P('scen', 'clus')
- bid: float32 [512, 96], P('scen')
- multiplier_next: float32 [512, 96], P('scen')
- node_mean: float32 [8, 96], replicated
- gap: float32 [], replicated
Inputs may be any that keep to these rules, and one draw needn't show every extreme that they name: `branch_of`: each of the 8 branches holds exactly 64 scenarios. `prob`: positive.
All inputs are finite; a program needn't handle non-finite values.
Results may differ from a plain program's by a relative error of at most 0.0035.
Values may be sent and summed in bfloat16 or wider, within the bound.
A program may use at most 64 MiB of HBM per device.

v0:
```python
import jax
import jax.numpy as jnp
from jax import lax
from jax.sharding import PartitionSpec as P


def node_statistics(weighted, masses, split_at):
    root_mean = jnp.sum(weighted, axis=0) / jnp.sum(masses)
    branch_mean = weighted / masses[:, None]
    columns = jnp.arange(weighted.shape[1], dtype=jnp.int32)
    return jnp.where((columns < split_at)[None, :], root_mean[None, :], branch_mean)


def solve_prices(schur, offset, mult, anchor, penalty):
    highest = lax.Precision.HIGHEST
    quarter = schur.shape[1]
    system = jnp.eye(quarter, dtype=jnp.float32)[None, :, :] + penalty * schur
    lower_fac = jnp.linalg.cholesky(system)
    right_hand = mult - penalty * (offset + anchor)
    prices = jax.vmap(
        lambda factor_one, side_one: jax.scipy.linalg.cho_solve((factor_one, True), side_one)
    )(lower_fac, right_hand)
    bid_part = -offset - jnp.einsum("stu,su->st", schur, prices, precision=highest)
    return (prices, bid_part)


def shards(
    factors,
    linear,
    arrival,
    departure,
    ev_count,
    prob,
    branch_of,
    multiplier,
    root_prev,
    branch_prev,
):
    highest = lax.Precision.HIGHEST
    scen_here = factors.shape[0]
    clus_here = factors.shape[1]
    block_width = linear.shape[2]
    quarter = multiplier.shape[1]
    split_at = root_prev.shape[0]
    branch_count = branch_prev.shape[0]
    clus_devices = lax.axis_size("clus")
    penalty = 1.0 / (clus_here * clus_devices)
    onehot = (branch_of[:, None] == jnp.arange(branch_count, dtype=jnp.int32)[None, :]).astype(
        jnp.float32
    )
    anchor_tail = jnp.dot(onehot, branch_prev, precision=highest)
    anchor = jnp.concatenate(
        [jnp.broadcast_to(root_prev[None, :], (scen_here, split_at)), anchor_tail], axis=1
    )
    hour_index = jnp.arange(quarter, dtype=jnp.int32)
    inside = ((hour_index >= arrival[..., None]) & (hour_index < departure[..., None])).astype(
        jnp.float32
    )
    scaled = inside * (ev_count.astype(jnp.float32) / 16.0)[None, :, None]
    effective_half = (linear * jnp.concatenate([scaled, scaled], axis=-1)).astype(jnp.bfloat16)
    blocks = factors.reshape(scen_here, clus_here, block_width, block_width)
    gram = jnp.einsum("sckt,scku->stu", blocks, blocks, preferred_element_type=jnp.float32)
    schur_local = (
        gram[:, :quarter, :quarter]
        - gram[:, :quarter, quarter:]
        - gram[:, quarter:, :quarter]
        + gram[:, quarter:, quarter:]
    )
    pushed = jnp.einsum("sckj,scj->sck", blocks, effective_half, preferred_element_type=jnp.float32)
    pushed_half = pushed.astype(jnp.bfloat16)
    back = jnp.einsum("sckj,sck->sj", blocks, pushed_half, preferred_element_type=jnp.float32)
    offset_local = back[:, :quarter] - back[:, quarter:]
    schur_sum, offset = lax.psum((schur_local, offset_local), "clus")
    prices, bid = solve_prices(schur_sum, offset, multiplier, anchor, penalty)
    prices_half = prices.astype(jnp.bfloat16)
    signed = jnp.concatenate([prices_half, -prices_half], axis=1)
    moved = pushed + jnp.einsum("sckj,sj->sck", blocks, signed, preferred_element_type=jnp.float32)
    moved_half = moved.astype(jnp.bfloat16)
    power = -jnp.einsum("sckj,sck->scj", blocks, moved_half, preferred_element_type=jnp.float32)
    weighted_local = jnp.einsum("sb,st->bt", onehot, prob[:, None] * bid, precision=highest)
    masses_local = jnp.einsum("sb,s->b", onehot, prob, precision=highest)
    weighted, masses = lax.psum((weighted_local, masses_local), "scen")
    node_mean = node_statistics(weighted, masses, split_at)
    target = jnp.dot(onehot, node_mean, precision=highest)
    distance = bid - target
    spread_local = jnp.sum(prob * jnp.sum(distance * distance, axis=1))
    spread_total = lax.psum(spread_local, "scen")
    gap = spread_total / (quarter * jnp.sum(masses))
    multiplier_next = multiplier + penalty * (bid - target)
    return (power, bid, multiplier_next, node_mean, gap)


def solution(mesh):
    return jax.shard_map(
        shards,
        mesh=mesh,
        in_specs=(
            P("scen", "clus", None),
            P("scen", "clus", None),
            P("scen", "clus"),
            P("scen", "clus"),
            P("clus"),
            P("scen"),
            P("scen"),
            P("scen", None),
            P(),
            P(),
        ),
        out_specs=(P("scen", "clus", None), P("scen", None), P("scen", None), P(), P()),
        check_vma=False,
    )
```

profile of v0, /device:TPU:1, one launch (start us, length us, event | category | flops | bytes accessed | tf_op | source)
XLA Modules:
  0.0 656.8 jit_solution(4997482680913107740)
XLA Ops:
  7.2 10.4 %reshape.56 = bf16[16,4,192,192]{3,2,1,0:T(8,128)(2,1)} reshape(bf16[16,4,36864]{2,1,0:T(4,128)(2,1)} %param.10) | data formatting | bytes 9437184 | tf_op jit(solution)/shard_map/reshape | solution.py:61
  17.6 6.5 convolution_bitcast_fusion
  24.1 1.3 slice_add_fusion
  26.0 4.6 fusion.10
  30.7 1.0 fusion.8
  31.9 40.4 %psum.36 = f32[16,96]{1,0:T(8,128)S(1)} all-reduce(f32[16,96]{1,0:T(8,128)S(1)} %slice_subtract_fusion.2), channel_id=1, replica_groups=mesh['scen'=32,'clus'=16] {'clus'}, use_global_device_ids=true, to_apply=%region_3.4 | all-reduce | flops 1536 | bytes 12288 | tf_op jit(solution)/shard_map/psum | solution.py:73
  72.8 116.6 %all-reduce.3.cloned.1.call-done = f32[16,96,96]{1,2,0:T(8,128)} async-done(((f32[16,96,96]{1,2,0:T(8,128)}), f32[16,96,96]{1,2,0:T(8,128)}) %all-reduce.3.cloned.1.call-update) | async-done | bytes 589840 | tf_op jit(solution)/shard_map/psum | solution.py:73
  189.4 1.3 multiply_add_fusion
  190.7 0.3 copy.32
  191.0 1.3 fusion.3
  192.3 140.7 %custom-call.11 = f32[16,96,96]{2,1,0:T(8,128)S(1)} custom-call(f32[16,96,96]{2,1,0:T(8,128)S(1)} %fusion.3), custom_call_target="Cholesky" | custom-call | tf_op jit(solution)/shard_map/jit(cholesky)/cholesky | solution.py:18
  333.4 117.9 %custom-call.12 = f32[16,1,96,96]{2,3,1,0:T(8,128)S(1)} custom-call(f32[16,1,96,96]{3,2,1,0:T(8,128)S(1)} %select_bitcast_fusion), custom_call_target="InvertDiagBlocksLowerTriangular" | custom-call | tf_op jit(solution)/shard_map/vmap(jit(_cho_solve))/triangular_solve | solution.py:21
  451.3 0.8 convolution_bitcast_fusion.1
  452.1 1.3 fusion
  453.4 0.8 fusion.22
  454.5 96.3 %all-reduce = (f32[8,96]{1,0:T(8,128)S(1)}, f32[8]{0:T(128)S(1)}) all-reduce(f32[8,96]{1,0:T(8,128)S(1)} %fusion.24, f32[8]{0:T(128)S(1)} %convolution_bitcast_fusion.2), channel_id=1, replica_groups=mesh['scen'=32,'clus'=16] {'scen'}, use_global_device_ids=true, to_apply=%region_4.5 | all-reduce | flops 776 | bytes 6208 | tf_op jit(solution)/shard_map/psum | solution.py:82
  550.8 0.6 reduce_sum.41
  551.4 0.6 broadcast_divide_fusion
  552.1 0.9 multiply_reduce_fusion
  553.1 0.6 multiply_reduce_fusion.1
  553.7 84.9 %psum.39 = f32[]{:T(128)} all-reduce(f32[]{:T(128)} %multiply_reduce_fusion.1), channel_id=1, replica_groups=mesh['scen'=32,'clus'=16] {'scen'}, use_global_device_ids=true, to_apply=%region_10.11 | all-reduce | flops 1 | bytes 8 | tf_op jit(solution)/shard_map/psum | solution.py:87
  639.3 4.5 fusion.17
  643.9 3.7 fusion.6
  647.6 0.7 bitcast_negate_fusion
  (55 shorter events, 2.1 us)
Async XLA Ops:
  7.2 65.3 %copy-start = (f32[8,64]{1,0:T(8,128)S(1)}, f32[8,64]{1,0:T(8,128)}, u32[]{:S(2)}) copy-start(f32[8,64]{1,0:T(8,128)} %param.19) | copy-start | bytes 6148
  7.2 182.3 %all-reduce.3.cloned.1.call-start = ((), (), s32[]{:S(2)}) async-start(), calls=%async_computation | async-start | bytes 1572864 | tf_op jit(solution)/shard_map/psum | solution.py:73
  17.6 8.0 %copy-start.7 = (s32[16,4]{0,1:T(4,128)S(1)}, s32[16,4]{0,1:T(4,128)}, u32[]{:S(2)}) copy-start(s32[16,4]{0,1:T(4,128)} %param.12) | copy-start | bytes 772
  17.6 8.0 %copy-start.8 = (s32[16,4]{0,1:T(4,128)S(1)}, s32[16,4]{0,1:T(4,128)}, u32[]{:S(2)}) copy-start(s32[16,4]{0,1:T(4,128)} %param.13) | copy-start | bytes 772
  17.6 8.1 %copy-start.9 = (s32[4]{0:T(128)S(1)}, s32[4]{0:T(128)}, u32[]{:S(2)}) copy-start(s32[4]{0:T(128)} %param.14) | copy-start | bytes 52
  17.6 8.2 %copy-start.3 = (f32[16,4,192]{2,1,0:T(4,128)S(1)}, f32[16,4,192]{2,1,0:T(4,128)}, u32[]{:S(2)}) copy-start(f32[16,4,192]{2,1,0:T(4,128)} %param.11) | copy-start | bytes 147460
  25.8 4.9 copy-start.1
  30.6 1.2 copy-start.10
  30.6 41.7 %copy-start.11 = (s32[16]{0:T(128)S(1)}, s32[16]{0:T(128)}, u32[]{:S(2)}) copy-start(s32[16]{0:T(128)} %param.16) | copy-start | bytes 196
  30.6 41.7 %copy-start.12 = (f32[16]{0:T(128)S(1)}, f32[16]{0:T(128)}, u32[]{:S(2)}) copy-start(f32[16]{0:T(128)} %param.15) | copy-start | bytes 196
  30.6 42.1 %copy-start.5 = (f32[16,96]{1,0:T(8,128)S(1)}, f32[16,96]{1,0:T(8,128)}, u32[]{:S(2)}) copy-start(f32[16,96]{1,0:T(8,128)} %param.17) | copy-start | bytes 18436
  189.4 264.0 %copy-start.2 = (f32[16,96,96]{1,2,0:T(8,128)S(1)}, f32[16,96,96]{1,2,0:T(8,128)}, u32[]{:S(2)}) copy-start(f32[16,96,96]{1,2,0:T(8,128)} %all-reduce.3.cloned.1.call-done) | copy-start | bytes 1769476
  454.3 193.3 %copy-start.4 = (f32[16,96]{1,0:T(8,128)}, f32[16,96]{1,0:T(8,128)S(1)}, u32[]{:S(2)}) copy-start(f32[16,96]{1,0:T(8,128)S(1)} %negate_subtract_fusion) | copy-start | bytes 18436
  552.1 95.4 %copy-start.6 = (f32[8,96]{1,0:T(8,128)}, f32[8,96]{1,0:T(8,128)S(1)}, u32[]{:S(2)}) copy-start(f32[8,96]{1,0:T(8,128)S(1)} %divide_select_fusion) | copy-start | bytes 9220
Sparse Core Ops, SparseCore 0:
  25.6 163.7 all-reduce.2
where the time goes:
time: 657 us
  other arithmetic  266 us (40%)
  blocking collectives  222 us (34%)
  waiting for transfers between devices  117 us (18%)
  matrix products  24.7 us (4%)
  between operations  16.6 us (3%)
  local copies, waits for them, and re-layouts  11 us (2%)
    another operation x4, other arithmetic, solve_prices(): lower_fac = jnp.linalg.cholesky(system)  141 us
    another operation x3, other arithmetic, solve_prices(): jax.scipy.linalg.cho_solve((factor_one, True), side_one)  118 us
    psum x1, waiting for transfers between devices, shards(): schur_sum, offset = lax.psum((schur_local, offset_local), 'clus')  117 us
    psum x1, blocking collectives, shards(): weighted, masses = lax.psum((weighted_local, masses_local), 'scen')  96.3 us
    psum x1, blocking collectives, shards(): spread_total = lax.psum(spread_local, 'scen')  84.9 us
    psum x1, blocking collectives, shards(): schur_sum, offset = lax.psum((schur_local, offset_local), 'clus')  40.4 us
  transfers between devices with their start and end apart: 1, of which 1 were waited for; matrix products, arithmetic and copies ran while one was open for 1% of the time, Pallas kernels for 0%

commit v1 on v0

v1 whole, which is shorter than its diff:
```python
import functools

import jax
import jax.numpy as jnp
from jax import lax
from jax.experimental import pallas as pl
from jax.experimental.pallas import tpu as pltpu
from jax.sharding import PartitionSpec as P

MESH = pl.DeviceIdType.MESH
HALVES = 2
LANES = 128
F32 = jnp.float32
BF16 = jnp.bfloat16


def iota(shape, axis):
    return lax.broadcasted_iota(jnp.int32, shape, axis)


def dot_nt(a, b):
    return lax.dot_general(a, b, (((1,), (1,)), ((), ())), preferred_element_type=F32)


def eliminate(system, quarter):
    lane = iota((1, LANES), 1)

    def trip(_, matrix):
        for p in range(8):
            row = matrix[p : p + 1, :]
            inv = 1.0 / row[:, p : p + 1]
            weight = jnp.where(lane == p, 1.0 - inv, row * inv)
            matrix = matrix - matrix[:, p : p + 1] * weight
        matrix = jnp.concatenate([matrix[8:quarter], matrix[:8], matrix[quarter:]], axis=0)
        return pltpu.roll(matrix, LANES - 8, 1)

    return lax.fori_loop(0, quarter // 8, trip, system)


def kernel(
    n_scen,
    n_clus,
    clus_here,
    quarter,
    split_at,
    branch_count,
    x_hbm,
    lin_ref,
    arr_ref,
    dep_ref,
    ev_ref,
    prob_ref,
    branch_ref,
    mult_ref,
    root_ref,
    bprev_ref,
    power_ref,
    bid_ref,
    next_ref,
    mean_ref,
    gap_ref,
    xbuf,
    pt_buf,
    push_buf,
    e_even,
    e_odd,
    lhs_even,
    lhs_odd,
    table,
    send_m,
    send_v,
    recv_m,
    recv_v,
    msg,
    recv_p,
    stat,
    recv_s,
    x_sem,
    sm_sem,
    sv_sem,
    rm_sem,
    rv_sem,
    sp_sem,
    rp_sem,
    ss_sem,
    rs_sem,
):
    scen_here = n_clus
    half = quarter // 2
    width = 2 * quarter
    rows = quarter * clus_here
    inner = n_scen // HALVES
    plane = HALVES * n_clus
    penalty = 1.0 / (clus_here * n_clus)
    g = lax.axis_index("scen")
    me = lax.axis_index("clus")
    my_half = g // inner
    my_inner = lax.rem(g, inner)
    my_slot = my_half * n_clus + me

    def x_copy(s, t):
        return pltpu.make_async_copy(x_hbm.at[s, :, t], xbuf.at[s, t], x_sem.at[s, t])

    def start_x(k, carry):
        s = lax.rem(me + 1 + k, n_clus)
        for t in range(3):
            x_copy(s, t).start()
        return carry

    lax.fori_loop(0, scen_here, start_x, 0)

    barrier = pltpu.get_barrier_semaphore()

    def plane_device(slot):
        return ((slot // n_clus) * inner + my_inner, lax.rem(slot, n_clus))

    def line_device(slot):
        return (my_half * inner + slot, me)

    def greet_plane(j, carry):
        pl.semaphore_signal(
            barrier, inc=1, device_id=plane_device(lax.rem(my_slot + j, plane)), device_id_type=MESH
        )
        return carry

    def greet_line(j, carry):
        pl.semaphore_signal(
            barrier, inc=1, device_id=line_device(lax.rem(my_inner + j, inner)), device_id_type=MESH
        )
        return carry

    lax.fori_loop(1, plane, greet_plane, 0)
    lax.fori_loop(1, inner, greet_line, 0)

    t_index = iota((quarter, 2 * LANES), 0)
    l_index = iota((quarter, 2 * LANES), 1)
    even = jnp.where(l_index == t_index, 1.0, 0.0) - jnp.where(l_index == t_index + quarter, 1.0, 0.0)
    shifted = t_index + LANES // 2
    odd = jnp.where(l_index == shifted, 1.0, 0.0) - jnp.where(l_index == shifted + quarter, 1.0, 0.0)
    lhs_even[0:quarter, :] = even.astype(BF16)
    lhs_odd[0:quarter, :] = odd.astype(BF16)

    lane2 = iota((8, 2 * LANES), 1)
    hour = jnp.where(lane2 < quarter, lane2, lane2 - quarter)
    sub2 = iota((8, 2 * LANES), 0)
    count = jnp.zeros((8, 2 * LANES), F32)
    for c in range(clus_here):
        count = jnp.where(sub2 == c, ev_ref[c].astype(F32) / 16.0, count)

    def costs(s, carry):
        first = jnp.zeros((8, 2 * LANES), jnp.int32)
        last = jnp.zeros((8, 2 * LANES), jnp.int32)
        for c in range(clus_here):
            first = jnp.where(sub2 == c, arr_ref[s, c], first)
            last = jnp.where(sub2 == c, dep_ref[s, c], last)
        inside = jnp.where((hour >= first) & (hour < last), 1.0, 0.0)
        scaled = inside * count
        cost = jnp.concatenate(
            [lin_ref[s], jnp.zeros((clus_here, 2 * LANES - width), F32)], axis=1
        )
        cost = jnp.concatenate([cost, jnp.zeros((8 - clus_here, 2 * LANES), F32)], axis=0)
        value = cost * scaled
        pad = jnp.zeros((8, 2 * LANES), F32)
        e_even[s] = jnp.concatenate([value, pad], axis=0).astype(BF16)
        turned = pltpu.roll(value, LANES // 2, 1)
        e_odd[s] = jnp.concatenate([turned, pad], axis=0).astype(BF16)
        return carry

    lax.fori_loop(0, scen_here, costs, 0)

    def m_copy(dest, slot, sem_slot):
        return pltpu.make_async_remote_copy(
            src_ref=send_m.at[dest],
            dst_ref=recv_m.at[slot],
            send_sem=sm_sem.at[dest],
            recv_sem=rm_sem.at[sem_slot],
            device_id=(g, dest),
            device_id_type=MESH,
        )

    def v_copy(dest, slot, sem_slot):
        return pltpu.make_async_remote_copy(
            src_ref=send_v.at[dest],
            dst_ref=recv_v.at[slot],
            send_sem=sv_sem.at[dest],
            recv_sem=rv_sem.at[sem_slot],
            device_id=(g, dest),
            device_id_type=MESH,
        )

    row_of = lax.rem(iota((8, rows), 1), clus_here) == iota((8, rows), 0)
    diag_of = iota((quarter, LANES), 0) == iota((quarter, LANES), 1)
    below = iota((half, LANES), 1) < iota((half, LANES), 0)

    def local(k, carry):
        s = lax.rem(me + 1 + k, n_clus)
        for t in range(3):
            x_copy(s, t).wait()
        a = xbuf[s, 0].reshape(rows, LANES)
        b = xbuf[s, 1].reshape(rows, LANES)
        c = xbuf[s, 2].reshape(rows, LANES)
        lhs_even[quarter : quarter + 16, :] = e_even[s]
        lhs_odd[quarter : quarter + 16, :] = e_odd[s]
        part_even = dot_nt(lhs_even[...], jnp.concatenate([a, b], axis=1))
        part_odd = dot_nt(lhs_odd[...], jnp.concatenate([b, c], axis=1))
        pushed_even = jnp.sum(
            jnp.where(row_of, part_even[quarter : quarter + 8], 0.0), axis=0, keepdims=True
        )
        pushed_odd = jnp.sum(
            jnp.where(row_of, part_odd[quarter : quarter + 8], 0.0), axis=0, keepdims=True
        )
        pushed = jnp.concatenate([pushed_even, pushed_odd], axis=1)
        push_buf[s] = pushed
        paired = jnp.concatenate([part_even[:quarter], part_odd[:quarter]], axis=1).astype(BF16)
        pt_buf[s] = paired
        pushed_rows = jnp.broadcast_to(pushed, (16, 2 * rows)).astype(BF16)
        left = jnp.concatenate([paired, pushed_rows], axis=0)
        right = jnp.concatenate([left, jnp.zeros((16, 2 * rows), BF16)], axis=0)
        product = dot_nt(left, right)
        schur = product[:quarter]
        low = pltpu.roll(schur[half:], LANES - half, 1)
        send_m[s] = jnp.where(below, low, schur[:half]).astype(BF16)
        send_v[s, 0:1, :] = product[quarter : quarter + 1]
        send_v[s, 1:2, :] = jnp.sum(jnp.where(diag_of, schur, 0.0), axis=0, keepdims=True)

        @pl.when(k == 0)
        def _():
            pl.semaphore_wait(barrier, plane - 1 + inner - 1)

        @pl.when(k < scen_here - 1)
        def _():
            m_copy(s, me, me).start()
            v_copy(s, me, me).start()

        return carry

    lax.fori_loop(0, scen_here, local, 0)

    def gather(j, carry):
        mat, vec = carry
        source = lax.rem(me + n_clus - j, n_clus)
        m_copy(source, source, source).wait_recv()
        v_copy(source, source, source).wait_recv()
        return (mat + recv_m[source].astype(F32), vec + recv_v[source])

    mat, vec = lax.fori_loop(1, n_clus, gather, (send_m[me].astype(F32), send_v[me]))

    lane_h = iota((half, LANES), 1)
    row_h = iota((half, LANES), 0)
    flipped = jnp.concatenate([mat, jnp.zeros((LANES - half, LANES), F32)], axis=0).T
    flip_a = flipped[:half]
    top = jnp.where(lane_h > row_h, mat, flip_a)
    low = jnp.where(lane_h < row_h, mat, flip_a)
    low = pltpu.roll(low, half, 1)
    bottom = jnp.where(lane_h < half, flipped[half:quarter], low)
    schur = jnp.concatenate([top, bottom], axis=0)
    lane_q = iota((quarter, LANES), 1)
    schur = jnp.where(diag_of, vec[1:2], schur)
    system = jnp.where(diag_of, 1.0 + penalty * schur, penalty * schur)
    system = jnp.where(lane_q < quarter, system, 0.0)

    lane1 = iota((1, LANES), 1)
    branch = branch_ref[me]
    table[...] = jnp.zeros((8, LANES), F32)
    table[:, 0:split_at] = jnp.broadcast_to(root_ref[...], (8, split_at))
    table[:, split_at:quarter] = bprev_ref[...]
    anchor = jnp.sum(
        jnp.where(iota((8, LANES), 0) == branch, table[...], 0.0), axis=0, keepdims=True
    )
    mult = jnp.concatenate(
        [mult_ref[pl.ds(me, 1), :], jnp.zeros((1, LANES - quarter), F32)], axis=1
    )
    side = jnp.where(lane1 < quarter, mult - penalty * (vec[0:1] + anchor), 0.0)
    side_rows = jnp.where(iota((8, LANES), 0) == 0, side, 0.0)
    solved = eliminate(jnp.concatenate([system, side_rows], axis=0), quarter)
    prices = pltpu.roll(solved[quarter:], quarter, 1)[0:1]
    bid = anchor + (prices - mult) / penalty
    msg[0:1, :] = prices
    tail = jnp.where(lane1 == quarter, prob_ref[me], jnp.where(lane1 == quarter + 1, branch.astype(F32), 0.0))
    msg[1:2, :] = jnp.where(lane1 < quarter, bid, tail)
    recv_p[my_slot] = msg[...]

    def p_copy(slot, at):
        return pltpu.make_async_remote_copy(
            src_ref=msg,
            dst_ref=recv_p.at[at],
            send_sem=sp_sem.at[slot],
            recv_sem=rp_sem.at[at],
            device_id=plane_device(slot),
            device_id_type=MESH,
        )

    def send_p(j, carry):
        p_copy(lax.rem(my_slot + j, plane), my_slot).start()
        return carry

    lax.fori_loop(1, plane, send_p, 0)

    def wait_p(j, carry):
        slot = lax.rem(my_slot + plane - j, plane)
        p_copy(slot, slot).wait_recv()
        return carry

    lax.fori_loop(1, plane, wait_p, 0)

    lane_p = iota((plane, LANES), 1)
    raw = recv_p[:, 1, :]
    chance = raw[:, quarter : quarter + 1]
    group = raw[:, quarter + 1 : quarter + 2]
    bids = jnp.where(lane_p < quarter, raw, jnp.where(lane_p == quarter, 1.0, 0.0))
    centre = jnp.zeros((plane, LANES), F32)
    for b in range(branch_count):
        member = group == float(b)
        total = jnp.sum(jnp.where(member, chance * bids, 0.0), axis=0, keepdims=True)
        mass = total[:, quarter : quarter + 1]
        mean = jnp.where(mass > 0.0, total / jnp.where(mass > 0.0, mass, 1.0), 0.0)
        centre = jnp.where(member, mean, centre)
        stat[b : b + 1, :] = total
    away = bids - centre
    stat[8:9, :] = jnp.sum(chance * (away * away), axis=0, keepdims=True)
    stat[9:16, :] = jnp.zeros((7, LANES), F32)
    recv_s[my_inner] = stat[...]

    def s_copy(slot, at):
        return pltpu.make_async_remote_copy(
            src_ref=stat,
            dst_ref=recv_s.at[at],
            send_sem=ss_sem.at[slot],
            recv_sem=rs_sem.at[at],
            device_id=line_device(slot),
            device_id_type=MESH,
        )

    def send_s(j, carry):
        s_copy(lax.rem(my_inner + j, inner), my_inner).start()
        return carry

    lax.fori_loop(1, inner, send_s, 0)

    def powers(s, carry):
        price = recv_p[my_half * n_clus + s, 0:1, :][:, :quarter]
        price = jnp.broadcast_to(price, (16, quarter)).astype(BF16)
        step = jnp.dot(price, pt_buf[s], preferred_element_type=F32)
        moved = push_buf[s] + step[0:1]
        stacked = jnp.concatenate(
            [
                jnp.where(row_of, moved[:, :rows], 0.0)[:clus_here],
                jnp.where(row_of, moved[:, rows:], 0.0)[:clus_here],
                jnp.zeros((16 - 2 * clus_here, rows), F32),
            ],
            axis=0,
        ).astype(BF16)
        blocks = jnp.concatenate([xbuf[s, t].reshape(rows, LANES) for t in range(3)], axis=1)
        out = jnp.dot(stacked, blocks, preferred_element_type=F32)
        from_odd = pltpu.roll(out[clus_here : 2 * clus_here, LANES:], LANES + LANES // 2, 1)
        total = out[:clus_here, : 2 * LANES] + from_odd
        power_ref[s] = -total[:, :width]
        return carry

    lax.fori_loop(0, scen_here, powers, 0)

    def wait_s(j, carry):
        slot = lax.rem(my_inner + inner - j, inner)
        s_copy(slot, slot).wait_recv()
        return carry

    lax.fori_loop(1, inner, wait_s, 0)

    lane8 = iota((8, LANES), 1)
    weighted = recv_s[0, 0:8, :]
    for j in range(1, inner):
        weighted = weighted + recv_s[j, 0:8, :]
    masses = weighted[:, quarter : quarter + 1]
    whole = jnp.sum(weighted, axis=0, keepdims=True)
    whole_mass = whole[:, quarter : quarter + 1]
    mean = jnp.where(lane8 < split_at, whole / whole_mass, weighted / masses)
    mean_ref[...] = mean[:, :quarter]
    spread = jnp.zeros((8, LANES), F32)
    within = jnp.zeros((1, LANES), F32)
    for j in range(inner):
        part = recv_s[j, 0:8, :]
        mass = part[:, quarter : quarter + 1]
        here = mass > 0.0
        away = jnp.where(here, part / jnp.where(here, mass, 1.0) - mean, 0.0)
        spread = spread + mass * (away * away)
        within = within + recv_s[j, 8:9, :]
    spread = jnp.where(lane8 < quarter, spread, 0.0)
    within = jnp.where(lane1 < quarter, within, 0.0)
    both = jnp.sum(spread, axis=0, keepdims=True) + within
    gap_ref[...] = jnp.sum(both, axis=1, keepdims=True) / (quarter * whole_mass)

    mine = recv_p[pl.ds(my_half * n_clus, n_clus), 1, :]
    group = mine[:, quarter + 1 : quarter + 2]
    target = jnp.zeros((n_clus, LANES), F32)
    for b in range(branch_count):
        target = jnp.where(group == float(b), mean[b : b + 1], target)
    bid_ref[...] = mine[:, :quarter]
    next_ref[...] = mult_ref[...] + penalty * (mine - target)[:, :quarter]

    def drain_m(j, carry):
        dest = lax.rem(me + j, n_clus)
        m_copy(dest, me, me).wait_send()
        v_copy(dest, me, me).wait_send()
        return carry

    def drain_p(j, carry):
        p_copy(lax.rem(my_slot + j, plane), my_slot).wait_send()
        return carry

    def drain_s(j, carry):
        s_copy(lax.rem(my_inner + j, inner), my_inner).wait_send()
        return carry

    lax.fori_loop(1, n_clus, drain_m, 0)
    lax.fori_loop(1, plane, drain_p, 0)
    lax.fori_loop(1, inner, drain_s, 0)


def solution(mesh):
    n_scen, n_clus = mesh.shape["scen"], mesh.shape["clus"]

    def step(
        factors,
        linear,
        arrival,
        departure,
        ev_count,
        prob,
        branch_of,
        multiplier,
        root_prev,
        branch_prev,
    ):
        scen_here, clus_here = factors.shape[:2]
        width = linear.shape[2]
        quarter = multiplier.shape[1]
        split_at = root_prev.shape[0]
        branch_count = branch_prev.shape[0]
        rows = quarter * clus_here
        plane = HALVES * n_clus
        inner = n_scen // HALVES
        tiles = factors.reshape(scen_here, clus_here, quarter, 3, LANES).transpose(0, 2, 3, 1, 4)
        vmem = pl.BlockSpec(memory_space=pltpu.VMEM)
        smem = pl.BlockSpec(memory_space=pltpu.SMEM)
        dma = pltpu.SemaphoreType.DMA
        power, bid, following, mean, gap = pl.pallas_call(
            functools.partial(
                kernel, n_scen, n_clus, clus_here, quarter, split_at, branch_count
            ),
            out_shape=(
                jax.ShapeDtypeStruct((scen_here, clus_here, width), F32),
                jax.ShapeDtypeStruct((scen_here, quarter), F32),
                jax.ShapeDtypeStruct((scen_here, quarter), F32),
                jax.ShapeDtypeStruct((branch_count, quarter), F32),
                jax.ShapeDtypeStruct((1, 1), F32),
            ),
            in_specs=[
                pl.BlockSpec(memory_space=pl.ANY),
                vmem,
                smem,
                smem,
                smem,
                smem,
                smem,
                vmem,
                vmem,
                vmem,
            ],
            out_specs=(vmem,) * 5,
            scratch_shapes=[
                pltpu.VMEM((scen_here, 3, quarter, clus_here, LANES), BF16),
                pltpu.VMEM((scen_here, quarter, 2 * rows), BF16),
                pltpu.VMEM((scen_here, 1, 2 * rows), F32),
                pltpu.VMEM((scen_here, 16, 2 * LANES), BF16),
                pltpu.VMEM((scen_here, 16, 2 * LANES), BF16),
                pltpu.VMEM((quarter + 16, 2 * LANES), BF16),
                pltpu.VMEM((quarter + 16, 2 * LANES), BF16),
                pltpu.VMEM((8, LANES), F32),
                pltpu.VMEM((n_clus, quarter // 2, LANES), BF16),
                pltpu.VMEM((n_clus, 2, LANES), F32),
                pltpu.VMEM((n_clus, quarter // 2, LANES), BF16),
                pltpu.VMEM((n_clus, 2, LANES), F32),
                pltpu.VMEM((2, LANES), F32),
                pltpu.VMEM((plane, 2, LANES), F32),
                pltpu.VMEM((16, LANES), F32),
                pltpu.VMEM((inner, 16, LANES), F32),
                dma((scen_here, 3)),
                dma((n_clus,)),
                dma((n_clus,)),
                dma((n_clus,)),
                dma((n_clus,)),
                dma((plane,)),
                dma((plane,)),
                dma((inner,)),
                dma((inner,)),
            ],
            compiler_params=pltpu.CompilerParams(collective_id=0, has_side_effects=True),
        )(
            tiles,
            linear,
            arrival,
            departure,
            ev_count,
            prob,
            branch_of,
            multiplier,
            root_prev[None, :],
            branch_prev,
        )
        return (power, bid, following, mean, gap.reshape(()))

    return jax.shard_map(
        step,
        mesh=mesh,
        in_specs=(
            P("scen", "clus", None),
            P("scen", "clus", None),
            P("scen", "clus"),
            P("scen", "clus"),
            P("clus"),
            P("scen"),
            P("scen"),
            P("scen", None),
            P(),
            P(),
        ),
        out_specs=(P("scen", "clus", None), P("scen", None), P("scen", None), P(), P()),
        check_vma=False,
    )
```

time: 657 us -> 64.7 us (0.10)
  other arithmetic: 266 us -> 0 us
  blocking collectives: 222 us -> 0 us
  waiting for transfers between devices: 117 us -> 0 us
  Pallas kernels: 0 us -> 53.9 us
  matrix products: 24.7 us -> 0 us
  between operations: 16.6 us -> 2.33 us
    another operation x7 -> x0, other arithmetic: 259 us -> none  [the longest x4 141 us: solve_prices(): lower_fac = jnp.linalg.cholesky(system)]
    psum x3 -> x0, blocking collectives: 222 us -> none  [the longest x1 96.3 us: shards(): weighted, masses = lax.psum((weighted_local, masses_local), 'scen')]
    psum x1 -> x0, waiting for transfers between devices: 117 us -> none  [shards(): schur_sum, offset = lax.psum((schur_local, offset_local), 'clus')]
    pallas_call x0 -> x1, Pallas kernels: none -> 53.9 us  [step(): pl.pallas_call(functools.partial(kernel, n_scen, n_clus, clus_here, quart...]
    dot_general x10 -> x0, matrix products: 22.6 us -> none  [the longest x1 6.5 us: shards(): jnp.einsum('sckt,scku->stu', blocks, blocks, preferred_element_type=jnp.f...]
    reshape x1 -> x0, local copies, waits for them, and re-layouts: 10.4 us -> none  [shards(): blocks = factors.reshape(scen_here, clus_here, block_width, block_width)]
    unnamed x28 -> x6, local copies, waits for them, and re-layouts: 0.25 us -> 8.05 us
  transfers between devices with their start and end apart: 1 -> 0, of which waited for: 1 -> 0; matrix products, arithmetic and copies ran while one was open for 1% -> 0% of each run, Pallas kernels for 0% -> 0%
where the time goes in v1:
time: 64.7 us; the launch traced here: 64.3 us
  Pallas kernels  53.9 us (83%)
  local copies, waits for them, and re-layouts  8.05 us (12%)
  between operations  2.33 us (4%)
    pallas_call x1, Pallas kernels, step(): pl.pallas_call(functools.partial(kernel, n_scen, n_clus, clus_here, quart...  53.9 us
    unnamed x6, local copies, waits for them, and re-layouts  8.05 us

profile of v1, /device:TPU:1, one launch (start us, length us, event | category | flops | bytes accessed | tf_op | source)
XLA Modules:
  0.0 64.3 jit_solution(17943872507300575262)
XLA Ops:
  0.6 1.4 %copy.15.arr_ref = s32[16,4]{1,0:T(8,128)} copy(s32[16,4]{0,1:T(4,128)} %param.12) | data formatting | bytes 512 | tf_op args[2]
  2.0 1.4 %copy.16.dep_ref = s32[16,4]{1,0:T(8,128)} copy(s32[16,4]{0,1:T(4,128)} %param.13) | data formatting | bytes 512 | tf_op args[3]
  3.3 53.9 %shard_map.137 = (f32[16,4,192]{2,1,0:T(4,128)}, f32[16,96]{1,0:T(8,128)}, f32[16,96]{1,0:T(8,128)}, f32[8,96]{1,0:T(8,128)}, f32[1,1]{1,0:T(1,128)}) custom-call(bf16[16,96,3,4,128]{4,3,2,1,0:T(4,128)(2,1)} %bitcast.5, f32[16,4,192]{2,1,0:T(4,128)} %lin_ref.1, s32[16,4]{1,0:T(8,128)} %copy.15.arr_ref, s32[16,4]{1,0:T(8,128)} %copy.16.dep_ref, s32[4]{0:T(128)} %ev_ref.1, ...), custom_call_target="tpu_custom_call" | custom-call | tf_op jit(solution)/shard_map/pallas_call | solution.py:446
  57.2 1.5 %copy.22 = f32[16,4,192]{2,1,0:T(4,128)} copy(f32[16,4,192]{2,1,0:T(4,128)} %get-tuple-element.20) | data formatting | bytes 98304
  58.7 1.3 %copy.23 = f32[16,96]{1,0:T(8,128)} copy(f32[16,96]{1,0:T(8,128)} %get-tuple-element.21) | data formatting | bytes 12288
  60.0 1.3 %copy.24 = f32[16,96]{1,0:T(8,128)} copy(f32[16,96]{1,0:T(8,128)} %get-tuple-element.22) | data formatting | bytes 12288
  61.3 1.3 %copy.25 = f32[8,96]{1,0:T(8,128)} copy(f32[8,96]{1,0:T(8,128)} %get-tuple-element.23) | data formatting | bytes 6144

commit v2 on v1

v2 whole, which is shorter than its diff:
```python
import functools

import jax
import jax.numpy as jnp
from jax import lax
from jax.experimental import pallas as pl
from jax.experimental.pallas import tpu as pltpu
from jax.sharding import PartitionSpec as P

MESH = pl.DeviceIdType.MESH
HALVES = 2
LANES = 128
F32 = jnp.float32
BF16 = jnp.bfloat16


def iota(shape, axis):
    return lax.broadcasted_iota(jnp.int32, shape, axis)


def dot_nt(a, b):
    return lax.dot_general(a, b, (((1,), (1,)), ((), ())), preferred_element_type=F32)


def spread_row(tile, p):
    return jnp.broadcast_to(tile[p : p + 1, :], (8, LANES))


def eliminate(system, quarter):
    height = quarter + 8
    lane = iota((8, LANES), 1)
    sub = iota((8, LANES), 0)
    lane_all = iota((height, LANES), 1)

    def trip(k, matrix):
        base = 8 * k
        columns = [
            jnp.take_along_axis(matrix, jnp.full((height, LANES), base + q, jnp.int32), axis=1)
            for q in range(8)
        ]
        block = matrix[:8]
        own = [column[:8] for column in columns]
        for p in range(8):
            here = sub == p
            inv = 1.0 / spread_row(own[p], p)
            factor = jnp.where(here, 0.0, own[p])
            for q in range(p + 1, 8):
                scaled = spread_row(own[q], p) * inv
                own[q] = jnp.where(here, scaled, own[q] - factor * scaled)
            scaled = spread_row(block, p) * inv
            block = jnp.where(here, scaled, block - factor * scaled)
            block = jnp.where(lane == base + p, jnp.where(here, inv, -own[p] * inv), block)
        weight = jnp.where((lane >= base) & (lane < base + 8), -block, block)
        taken = (lane_all >= base) & (lane_all < base + 8)
        terms = [
            columns[q] * jnp.broadcast_to(weight[q : q + 1, :], (height, LANES)) for q in range(8)
        ]
        while len(terms) > 1:
            terms = [terms[i] + terms[i + 1] for i in range(0, len(terms), 2)]
        matrix = jnp.where(taken, 0.0, matrix) - terms[0]
        return jnp.concatenate([matrix[8:quarter], matrix[:8], matrix[quarter:]], axis=0)

    return lax.fori_loop(0, quarter // 8, trip, system)


def kernel(
    n_scen,
    n_clus,
    clus_here,
    quarter,
    split_at,
    branch_count,
    x_hbm,
    lin_hbm,
    arr_hbm,
    dep_hbm,
    ev_hbm,
    prob_hbm,
    branch_hbm,
    mult_hbm,
    root_hbm,
    bprev_hbm,
    power_ref,
    bid_ref,
    next_ref,
    mean_ref,
    gap_ref,
    xbuf,
    lin_ref,
    arr_ref,
    dep_ref,
    ev_ref,
    prob_ref,
    branch_ref,
    mult_ref,
    root_ref,
    bprev_ref,
    pt_buf,
    push_buf,
    lhs_even,
    lhs_odd,
    table,
    chance,
    send_m,
    send_v,
    recv_m,
    recv_v,
    send_t,
    recv_t,
    msg,
    recv_p,
    stat,
    recv_s,
    small_sem,
    x_sem,
    send_sem,
    recv_sem,
):
    scen_here = n_clus
    half = quarter // 2
    width = 2 * quarter
    rows = quarter * clus_here
    inner = n_scen // HALVES
    plane = HALVES * n_clus
    penalty = 1.0 / (clus_here * n_clus)
    g = lax.axis_index("scen")
    me = lax.axis_index("clus")
    my_half = g // inner
    my_inner = lax.rem(g, inner)
    my_slot = my_half * n_clus + me
    my_base = my_half * n_clus
    other = 1 - my_half

    barrier = pltpu.get_barrier_semaphore()

    def plane_device(slot):
        return ((slot // n_clus) * inner + my_inner, lax.rem(slot, n_clus))

    def line_device(slot):
        return (my_half * inner + slot, me)

    def greet_plane(j, carry):
        pl.semaphore_signal(
            barrier, inc=1, device_id=plane_device(lax.rem(my_slot + j, plane)), device_id_type=MESH
        )
        return carry

    def greet_line(j, carry):
        pl.semaphore_signal(
            barrier, inc=1, device_id=line_device(lax.rem(my_inner + j, inner)), device_id_type=MESH
        )
        return carry

    small = [
        pltpu.make_async_copy(source, target, small_sem.at[i])
        for i, (source, target) in enumerate(
            (
                (lin_hbm, lin_ref),
                (arr_hbm, arr_ref),
                (dep_hbm, dep_ref),
                (ev_hbm, ev_ref),
                (prob_hbm, prob_ref),
                (branch_hbm, branch_ref),
                (mult_hbm, mult_ref),
                (root_hbm, root_ref),
                (bprev_hbm, bprev_ref),
            )
        )
    ]
    for copy in small:
        copy.start()

    def x_copy(s, t):
        return pltpu.make_async_copy(x_hbm.at[s, :, t], xbuf.at[s, t], x_sem.at[s, t])

    def start_x(k, carry):
        s = lax.rem(me + 1 + k, n_clus)
        for t in range(3):
            x_copy(s, t).start()
        return carry

    lax.fori_loop(0, scen_here, start_x, 0)
    lax.fori_loop(1, plane, greet_plane, 0)
    lax.fori_loop(1, inner, greet_line, 0)

    t_index = iota((quarter, 2 * LANES), 0)
    l_index = iota((quarter, 2 * LANES), 1)
    even = jnp.where(l_index == t_index, 1.0, 0.0) - jnp.where(l_index == t_index + quarter, 1.0, 0.0)
    shifted = t_index + LANES // 2
    odd = jnp.where(l_index == shifted, 1.0, 0.0) - jnp.where(l_index == shifted + quarter, 1.0, 0.0)
    lhs_even[...] = even.astype(BF16)
    lhs_odd[...] = odd.astype(BF16)

    for copy in small:
        copy.wait()

    lane2 = iota((8, 2 * LANES), 1)
    hour = jnp.where(lane2 < quarter, lane2, lane2 - quarter)
    sub2 = iota((8, 2 * LANES), 0)
    count = jnp.zeros((8, 2 * LANES), F32)
    for c in range(clus_here):
        count = jnp.where(sub2 == c, ev_ref[c].astype(F32) / 16.0, count)

    def costs(s):
        first = jnp.zeros((8, 2 * LANES), jnp.int32)
        last = jnp.zeros((8, 2 * LANES), jnp.int32)
        for c in range(clus_here):
            first = jnp.where(sub2 == c, arr_ref[c, s], first)
            last = jnp.where(sub2 == c, dep_ref[c, s], last)
        inside = jnp.where((hour >= first) & (hour < last), 1.0, 0.0)
        cost = jnp.concatenate(
            [lin_ref[s], jnp.zeros((clus_here, 2 * LANES - width), F32)], axis=1
        )
        cost = jnp.concatenate([cost, jnp.zeros((8 - clus_here, 2 * LANES), F32)], axis=0)
        value = cost * (inside * count)
        turned = pltpu.roll(value, LANES // 2, 1)
        pad = jnp.zeros((8, 2 * LANES), F32)
        return (
            jnp.concatenate([value, pad], axis=0).astype(BF16),
            jnp.concatenate([turned, pad], axis=0).astype(BF16),
        )

    def remote(source, target, kind, device):
        return pltpu.make_async_remote_copy(
            src_ref=source,
            dst_ref=target,
            send_sem=send_sem.at[kind],
            recv_sem=recv_sem.at[kind],
            device_id=device,
            device_id_type=MESH,
        )

    def await_all(buffer, kind, sems, amount):
        view = buffer.at[pl.ds(0, amount)]
        pltpu.make_async_copy(view, view, sems.at[kind]).wait()

    row_of = lax.rem(iota((8, rows), 1), clus_here) == iota((8, rows), 0)
    diag_of = iota((quarter, LANES), 0) == iota((quarter, LANES), 1)
    below = iota((half, LANES), 1) < iota((half, LANES), 0)
    lane1 = iota((1, LANES), 1)
    lane8 = iota((8, LANES), 1)
    sub8 = iota((8, LANES), 0)

    def tiles_of(s):
        return [xbuf.at[s, t].reshape(rows, LANES)[...] for t in range(3)]

    chances = jnp.zeros((1, LANES), F32)
    groups = jnp.zeros((1, LANES), F32)
    group_rows = jnp.zeros((n_clus, LANES), jnp.int32)
    sub_n = iota((n_clus, LANES), 0)
    for i in range(n_clus):
        chances = jnp.where(lane1 == i, prob_ref[i], chances)
        groups = jnp.where(lane1 == i, branch_ref[i].astype(F32), groups)
        group_rows = jnp.where(sub_n == i, branch_ref[i], group_rows)
        chance[my_base + i] = jnp.where(sub8 == branch_ref[i], prob_ref[i], 0.0)
    send_t[0:1, :] = chances
    send_t[1:2, :] = groups
    t_copy = remote(send_t, recv_t, 2, (other * inner + my_inner, me))

    def local(k, carry):
        s = lax.rem(me + 1 + k, n_clus)
        for t in range(3):
            x_copy(s, t).wait()
        a, b, c = tiles_of(s)
        cost_even, cost_odd = costs(s)
        part_even = dot_nt(
            jnp.concatenate([lhs_even[...], cost_even], axis=0), jnp.concatenate([a, b], axis=1)
        )
        part_odd = dot_nt(
            jnp.concatenate([lhs_odd[...], cost_odd], axis=0), jnp.concatenate([b, c], axis=1)
        )
        pushed_even = jnp.sum(
            jnp.where(row_of, part_even[quarter : quarter + 8], 0.0), axis=0, keepdims=True
        )
        pushed_odd = jnp.sum(
            jnp.where(row_of, part_odd[quarter : quarter + 8], 0.0), axis=0, keepdims=True
        )
        pushed = jnp.concatenate([pushed_even, pushed_odd], axis=1)
        push_buf[s] = pushed
        paired = jnp.concatenate([part_even[:quarter], part_odd[:quarter]], axis=1).astype(BF16)
        pt_buf[s] = paired
        pushed_rows = jnp.broadcast_to(pushed, (16, 2 * rows)).astype(BF16)
        left = jnp.concatenate([paired, pushed_rows], axis=0)
        right = jnp.concatenate([left, jnp.zeros((16, 2 * rows), BF16)], axis=0)
        product = dot_nt(left, right)
        schur = product[:quarter]
        low = pltpu.roll(schur[half:], LANES - half, 1)
        send_m[s] = jnp.where(below, low, schur[:half]).astype(BF16)
        send_v[s, 0:1, :] = product[quarter : quarter + 1]
        send_v[s, 1:2, :] = jnp.sum(jnp.where(diag_of, schur, 0.0), axis=0, keepdims=True)

        @pl.when(k == 0)
        def _():
            pl.semaphore_wait(barrier, plane - 1 + inner - 1)
            t_copy.start()

        @pl.when(k < scen_here - 1)
        def _():
            remote(send_m.at[s], recv_m.at[me], 0, (g, s)).start()
            remote(send_v.at[s], recv_v.at[me], 1, (g, s)).start()

        return carry

    lax.fori_loop(0, scen_here, local, 0)

    table[...] = jnp.zeros((8, LANES), F32)
    table[:, 0:split_at] = jnp.broadcast_to(root_ref[...], (8, split_at))
    table[:, split_at:quarter] = bprev_ref[...]
    branch = branch_ref[me]
    anchor = jnp.sum(jnp.where(sub8 == branch, table[...], 0.0), axis=0, keepdims=True)
    mult = jnp.concatenate(
        [mult_ref[pl.ds(me, 1), :], jnp.zeros((1, LANES - quarter), F32)], axis=1
    )
    t_copy.wait_recv()
    far_chance = recv_t[0:1, :]
    far_group = recv_t[1:2, :]
    for i in range(n_clus):
        member = sub8.astype(F32) == far_group[:, i : i + 1]
        chance[other * n_clus + i] = jnp.where(member, far_chance[:, i : i + 1], 0.0)
    mass = chance[0]
    for i in range(1, plane):
        mass = mass + chance[i]
    inv_mass = jnp.where(mass > 0.0, 1.0 / jnp.where(mass > 0.0, mass, 1.0), 0.0)

    recv_m[me] = send_m[me]
    recv_v[me] = send_v[me]
    await_all(recv_m, 0, recv_sem, n_clus - 1)
    await_all(recv_v, 1, recv_sem, n_clus - 1)
    mats = [recv_m[j].astype(F32) for j in range(n_clus)]
    vecs = [recv_v[j] for j in range(n_clus)]
    while len(mats) > 1:
        mats = [mats[i] + mats[i + 1] for i in range(0, len(mats), 2)]
        vecs = [vecs[i] + vecs[i + 1] for i in range(0, len(vecs), 2)]
    mat, vec = mats[0], vecs[0]

    lane_h = iota((half, LANES), 1)
    row_h = iota((half, LANES), 0)
    flipped = jnp.concatenate([mat, jnp.zeros((LANES - half, LANES), F32)], axis=0).T
    flip_a = flipped[:half]
    top = jnp.where(lane_h > row_h, mat, flip_a)
    low = jnp.where(lane_h < row_h, mat, flip_a)
    low = pltpu.roll(low, half, 1)
    bottom = jnp.where(lane_h < half, flipped[half:quarter], low)
    schur = jnp.concatenate([top, bottom], axis=0)
    lane_q = iota((quarter, LANES), 1)
    schur = jnp.where(diag_of, vec[1:2], schur)
    system = jnp.where(diag_of, 1.0 + penalty * schur, penalty * schur)
    system = jnp.where(lane_q < quarter, system, 0.0)
    side = jnp.where(lane1 < quarter, mult - penalty * (vec[0:1] + anchor), 0.0)
    side_rows = jnp.where(sub8 == 0, side, 0.0)
    solved = eliminate(jnp.concatenate([system, side_rows], axis=0), quarter)
    prices = solved[quarter : quarter + 1]
    bid = anchor + (prices - mult) / penalty
    msg[0:1, :] = prices
    msg[1:2, :] = jnp.where(lane1 < quarter, bid, jnp.where(lane1 == quarter, 1.0, 0.0))
    recv_p[my_slot] = msg[...]

    def send_p(j, carry):
        slot = lax.rem(my_slot + j, plane)
        remote(msg, recv_p.at[my_slot], 3, plane_device(slot)).start()
        return carry

    lax.fori_loop(1, plane, send_p, 0, unroll=True)
    await_all(recv_p, 3, recv_sem, plane - 1)

    def bid_tile(i):
        return jnp.broadcast_to(recv_p[i, 1:2, :], (8, LANES))

    totals = [chance[i] * bid_tile(i) for i in range(plane)]
    while len(totals) > 1:
        totals = [totals[i] + totals[i + 1] for i in range(0, len(totals), 2)]
    mean = totals[0] * inv_mass
    squares = []
    for i in range(plane):
        away = bid_tile(i) - mean
        squares.append(chance[i] * (away * away))
    while len(squares) > 1:
        squares = [squares[i] + squares[i + 1] for i in range(0, len(squares), 2)]
    square = jnp.sum(jnp.where(lane8 < quarter, squares[0], 0.0), axis=0, keepdims=True)
    square = jnp.sum(square, axis=1, keepdims=True)
    stat[...] = jnp.where(
        lane8 < quarter, mean, jnp.where(lane8 == quarter, mass, jnp.where(sub8 == 0, square, 0.0))
    )
    recv_s[my_inner] = stat[...]

    def send_s(j, carry):
        slot = lax.rem(my_inner + j, inner)
        remote(stat, recv_s.at[my_inner], 4, line_device(slot)).start()
        return carry

    lax.fori_loop(1, inner, send_s, 0, unroll=True)

    def powers(s, carry):
        price = recv_p[my_base + s, 0:1, :][:, :quarter]
        price = jnp.broadcast_to(price, (16, quarter)).astype(BF16)
        step = jnp.dot(price, pt_buf[s], preferred_element_type=F32)
        moved = push_buf[s] + step[0:1]
        stacked = jnp.concatenate(
            [
                jnp.where(row_of, moved[:, :rows], 0.0)[:clus_here],
                jnp.where(row_of, moved[:, rows:], 0.0)[:clus_here],
                jnp.zeros((16 - 2 * clus_here, rows), F32),
            ],
            axis=0,
        ).astype(BF16)
        out = jnp.dot(stacked, jnp.concatenate(tiles_of(s), axis=1), preferred_element_type=F32)
        from_odd = pltpu.roll(out[clus_here : 2 * clus_here, LANES:], LANES + LANES // 2, 1)
        total = out[:clus_here, : 2 * LANES] + from_odd
        power_ref[s] = -total[:, :width]
        return carry

    lax.fori_loop(0, scen_here, powers, 0, unroll=2)
    mine = recv_p[pl.ds(my_base, n_clus), 1, :]
    bid_ref[...] = mine[:, :quarter]
    await_all(send_m, 0, send_sem, n_clus - 1)
    await_all(send_v, 1, send_sem, n_clus - 1)
    t_copy.wait_send()
    await_all(recv_p, 3, send_sem, plane - 1)

    await_all(recv_s, 4, recv_sem, inner - 1)
    parts = [recv_s[j] for j in range(inner)]
    weights = [jnp.broadcast_to(part[:, quarter : quarter + 1], (8, LANES)) for part in parts]
    sums = [part * weight for part, weight in zip(parts, weights)]
    heavy = list(weights)
    while len(sums) > 1:
        sums = [sums[i] + sums[i + 1] for i in range(0, len(sums), 2)]
        heavy = [heavy[i] + heavy[i + 1] for i in range(0, len(heavy), 2)]
    whole = jnp.sum(sums[0], axis=0, keepdims=True)
    whole_mass = jnp.sum(heavy[0], axis=0, keepdims=True)
    node = jnp.where(lane8 < split_at, whole / whole_mass, sums[0] / heavy[0])
    mean_ref[...] = node[:, :quarter]
    target = jnp.zeros((n_clus, LANES), F32)
    for b in range(branch_count):
        target = jnp.where(group_rows == b, node[b : b + 1], target)
    next_ref[...] = mult_ref[...] + penalty * (mine - target)[:, :quarter]
    spread = []
    within = []
    for part, weight in zip(parts, weights):
        away = part - node
        spread.append(weight * (away * away))
        within.append(part[0:1])
    while len(spread) > 1:
        spread = [spread[i] + spread[i + 1] for i in range(0, len(spread), 2)]
        within = [within[i] + within[i + 1] for i in range(0, len(within), 2)]
    both = jnp.sum(jnp.where(lane8 < quarter, spread[0], 0.0), axis=0, keepdims=True)
    both = both + jnp.where(lane1 == quarter + 1, within[0], 0.0)
    gap_ref[...] = jnp.sum(both, axis=1, keepdims=True) / (quarter * whole_mass[:, 0:1])
    await_all(recv_s, 4, send_sem, inner - 1)


def solution(mesh):
    n_scen, n_clus = mesh.shape["scen"], mesh.shape["clus"]

    def step(
        factors,
        linear,
        arrival,
        departure,
        ev_count,
        prob,
        branch_of,
        multiplier,
        root_prev,
        branch_prev,
    ):
        scen_here, clus_here = factors.shape[:2]
        width = linear.shape[2]
        quarter = multiplier.shape[1]
        split_at = root_prev.shape[0]
        branch_count = branch_prev.shape[0]
        rows = quarter * clus_here
        plane = HALVES * n_clus
        inner = n_scen // HALVES
        tiles = factors.reshape(scen_here, clus_here, quarter, 3, LANES).transpose(0, 2, 3, 1, 4)
        vmem = pl.BlockSpec(memory_space=pltpu.VMEM)
        dma = pltpu.SemaphoreType.DMA
        power, bid, following, mean, gap = pl.pallas_call(
            functools.partial(
                kernel, n_scen, n_clus, clus_here, quarter, split_at, branch_count
            ),
            out_shape=(
                jax.ShapeDtypeStruct((scen_here, clus_here, width), F32),
                jax.ShapeDtypeStruct((scen_here, quarter), F32),
                jax.ShapeDtypeStruct((scen_here, quarter), F32),
                jax.ShapeDtypeStruct((branch_count, quarter), F32),
                jax.ShapeDtypeStruct((1, 1), F32),
            ),
            in_specs=[pl.BlockSpec(memory_space=pl.ANY)] * 10,
            out_specs=(vmem,) * 5,
            scratch_shapes=[
                pltpu.VMEM((scen_here, 3, quarter, clus_here, LANES), BF16),
                pltpu.VMEM(linear.shape, F32),
                pltpu.SMEM((clus_here, scen_here), jnp.int32),
                pltpu.SMEM((clus_here, scen_here), jnp.int32),
                pltpu.SMEM((clus_here,), jnp.int32),
                pltpu.SMEM((scen_here,), F32),
                pltpu.SMEM((scen_here,), jnp.int32),
                pltpu.VMEM(multiplier.shape, F32),
                pltpu.VMEM((1, split_at), F32),
                pltpu.VMEM(branch_prev.shape, F32),
                pltpu.VMEM((scen_here, quarter, 2 * rows), BF16),
                pltpu.VMEM((scen_here, 1, 2 * rows), F32),
                pltpu.VMEM((quarter, 2 * LANES), BF16),
                pltpu.VMEM((quarter, 2 * LANES), BF16),
                pltpu.VMEM((8, LANES), F32),
                pltpu.VMEM((plane, 8, LANES), F32),
                pltpu.VMEM((n_clus, quarter // 2, LANES), BF16),
                pltpu.VMEM((n_clus, 2, LANES), F32),
                pltpu.VMEM((n_clus, quarter // 2, LANES), BF16),
                pltpu.VMEM((n_clus, 2, LANES), F32),
                pltpu.VMEM((2, LANES), F32),
                pltpu.VMEM((2, LANES), F32),
                pltpu.VMEM((2, LANES), F32),
                pltpu.VMEM((plane, 2, LANES), F32),
                pltpu.VMEM((8, LANES), F32),
                pltpu.VMEM((inner, 8, LANES), F32),
                dma((9,)),
                dma((scen_here, 3)),
                dma((5,)),
                dma((5,)),
            ],
            compiler_params=pltpu.CompilerParams(collective_id=0, has_side_effects=True),
        )(
            tiles,
            linear,
            arrival.T,
            departure.T,
            ev_count,
            prob,
            branch_of,
            multiplier,
            root_prev[None, :],
            branch_prev,
        )
        return (power, bid, following, mean, gap.reshape(()))

    return jax.shard_map(
        step,
        mesh=mesh,
        in_specs=(
            P("scen", "clus", None),
            P("scen", "clus", None),
            P("scen", "clus"),
            P("scen", "clus"),
            P("clus"),
            P("scen"),
            P("scen"),
            P("scen", None),
            P(),
            P(),
        ),
        out_specs=(P("scen", "clus", None), P("scen", None), P("scen", None), P(), P()),
        check_vma=False,
    )
```

time: 64.7 us -> 51 us (0.79)
  Pallas kernels: 53.9 us -> 43.1 us
  local copies, waits for them, and re-layouts: 8.05 us -> 5.34 us
    pallas_call x1, Pallas kernels: 53.9 us -> 43.1 us  [step(): pl.pallas_call(functools.partial(kernel, n_scen, n_clus, clus_here, quart...]
    unnamed x6 -> x4, local copies, waits for them, and re-layouts: 8.05 us -> 5.34 us
where the time goes in v2:
time: 51 us; the launch traced here: 50.7 us
  Pallas kernels  43.1 us (85%)
  local copies, waits for them, and re-layouts  5.34 us (10%)
  between operations  2.33 us (5%)
    pallas_call x1, Pallas kernels, step(): pl.pallas_call(functools.partial(kernel, n_scen, n_clus, clus_here, quart...  43.1 us
    unnamed x4, local copies, waits for them, and re-layouts  5.34 us

profile of v2, /device:TPU:1, one launch (start us, length us, event | category | flops | bytes accessed | tf_op | source)
XLA Modules:
  0.0 50.7 jit_solution(11309791209539824638)
XLA Ops:
  0.6 43.1 %shard_map.137 = (f32[16,4,192]{2,1,0:T(4,128)}, f32[16,96]{1,0:T(8,128)}, f32[16,96]{1,0:T(8,128)}, f32[8,96]{1,0:T(8,128)}, f32[1,1]{1,0:T(1,128)}) custom-call(bf16[16,96,3,4,128]{4,3,2,1,0:T(4,128)(2,1)} %bitcast.7, f32[16,4,192]{2,1,0:T(4,128)} %lin_hbm.1, s32[4,16]{1,0:T(4,128)} %bitcast.8, s32[4,16]{1,0:T(4,128)} %bitcast.9, s32[4]{0:T(128)} %ev_hbm.1, ...), custom_call_target="tpu_custom_call" | custom-call | tf_op jit(solution)/shard_map/pallas_call | solution.py:477
  43.7 1.5 %copy.20 = f32[16,4,192]{2,1,0:T(4,128)} copy(f32[16,4,192]{2,1,0:T(4,128)} %get-tuple-element.20) | data formatting | bytes 98304
  45.2 1.3 %copy.21 = f32[16,96]{1,0:T(8,128)} copy(f32[16,96]{1,0:T(8,128)} %get-tuple-element.21) | data formatting | bytes 12288
  46.5 1.3 %copy.22 = f32[16,96]{1,0:T(8,128)} copy(f32[16,96]{1,0:T(8,128)} %get-tuple-element.22) | data formatting | bytes 12288
  47.8 1.3 %copy.23 = f32[8,96]{1,0:T(8,128)} copy(f32[8,96]{1,0:T(8,128)} %get-tuple-element.23) | data formatting | bytes 6144

commit v3 on v2

--- a/solution.py
+++ b/solution.py
@@ -170,13 +170,11 @@
     for copy in small:
         copy.start()
 
-    def x_copy(s, t):
-        return pltpu.make_async_copy(x_hbm.at[s, :, t], xbuf.at[s, t], x_sem.at[s, t])
+    def x_copy(s):
+        return pltpu.make_async_copy(x_hbm.at[s], xbuf.at[s], x_sem.at[s])
 
     def start_x(k, carry):
-        s = lax.rem(me + 1 + k, n_clus)
-        for t in range(3):
-            x_copy(s, t).start()
+        x_copy(lax.rem(me + 1 + k, n_clus)).start()
         return carry
 
     lax.fori_loop(0, scen_here, start_x, 0)
@@ -241,8 +239,17 @@
     lane8 = iota((8, LANES), 1)
     sub8 = iota((8, LANES), 0)
 
+    place = iota((rows // 16, 16, LANES), 1) // 4
+
     def tiles_of(s):
-        return [xbuf.at[s, t].reshape(rows, LANES)[...] for t in range(3)]
+        groups = xbuf[s].reshape(rows // 16, 48, LANES)
+        first, second, third = groups[:, :16], groups[:, 16:32], groups[:, 32:]
+        a = jnp.where(place == 2, second, jnp.where(place == 1, third, first))
+        b = jnp.where(place == 1, first, jnp.where(place == 2, third, second))
+        c = jnp.where(place == 2, first, jnp.where(place == 1, second, third))
+        b = jnp.concatenate([b[:, 4:], b[:, :4]], axis=1)
+        c = jnp.concatenate([c[:, 8:], c[:, :8]], axis=1)
+        return [tile.reshape(rows, LANES) for tile in (a, b, c)]
 
     chances = jnp.zeros((1, LANES), F32)
     groups = jnp.zeros((1, LANES), F32)
@@ -259,8 +266,7 @@
 
     def local(k, carry):
         s = lax.rem(me + 1 + k, n_clus)
-        for t in range(3):
-            x_copy(s, t).wait()
+        x_copy(s).wait()
         a, b, c = tiles_of(s)
         cost_even, cost_odd = costs(s)
         part_even = dot_nt(
@@ -448,6 +454,12 @@
     await_all(recv_s, 4, send_sem, inner - 1)
 
 
+def hand_out(*refs):
+    count = len(refs) // 2
+    for source, target in zip(refs[:count], refs[count:]):
+        target[...] = source[...]
+
+
 def solution(mesh):
     n_scen, n_clus = mesh.shape["scen"], mesh.shape["clus"]
 
@@ -471,24 +483,26 @@
         rows = quarter * clus_here
         plane = HALVES * n_clus
         inner = n_scen // HALVES
-        tiles = factors.reshape(scen_here, clus_here, quarter, 3, LANES).transpose(0, 2, 3, 1, 4)
+        tiles = factors.reshape(scen_here, clus_here, 3 * quarter, LANES)
+        tiles = tiles.transpose(0, 2, 1, 3).reshape(scen_here, 3 * rows, LANES)
         vmem = pl.BlockSpec(memory_space=pltpu.VMEM)
         dma = pltpu.SemaphoreType.DMA
-        power, bid, following, mean, gap = pl.pallas_call(
+        shapes = (
+            jax.ShapeDtypeStruct((scen_here, clus_here, width), F32),
+            jax.ShapeDtypeStruct((scen_here, quarter), F32),
+            jax.ShapeDtypeStruct((scen_here, quarter), F32),
+            jax.ShapeDtypeStruct((branch_count, quarter), F32),
+            jax.ShapeDtypeStruct((1, 1), F32),
+        )
+        results = pl.pallas_call(
             functools.partial(
                 kernel, n_scen, n_clus, clus_here, quarter, split_at, branch_count
             ),
-            out_shape=(
-                jax.ShapeDtypeStruct((scen_here, clus_here, width), F32),
-                jax.ShapeDtypeStruct((scen_here, quarter), F32),
-                jax.ShapeDtypeStruct((scen_here, quarter), F32),
-                jax.ShapeDtypeStruct((branch_count, quarter), F32),
-                jax.ShapeDtypeStruct((1, 1), F32),
-            ),
+            out_shape=shapes,
             in_specs=[pl.BlockSpec(memory_space=pl.ANY)] * 10,
             out_specs=(vmem,) * 5,
             scratch_shapes=[
-                pltpu.VMEM((scen_here, 3, quarter, clus_here, LANES), BF16),
+                pltpu.VMEM((scen_here, 3 * rows, LANES), BF16),
                 pltpu.VMEM(linear.shape, F32),
                 pltpu.SMEM((clus_here, scen_here), jnp.int32),
                 pltpu.SMEM((clus_here, scen_here), jnp.int32),
@@ -515,7 +529,7 @@
                 pltpu.VMEM((8, LANES), F32),
                 pltpu.VMEM((inner, 8, LANES), F32),
                 dma((9,)),
-                dma((scen_here, 3)),
+                dma((scen_here,)),
                 dma((5,)),
                 dma((5,)),
             ],
@@ -532,6 +546,9 @@
             root_prev[None, :],
             branch_prev,
         )
+        power, bid, following, mean, gap = pl.pallas_call(
+            hand_out, out_shape=shapes, in_specs=[vmem] * 5, out_specs=(vmem,) * 5
+        )(*results)
         return (power, bid, following, mean, gap.reshape(()))
 
     return jax.shard_map(

time: 51 us -> 45.7 us (0.90)
  local copies, waits for them, and re-layouts: 5.34 us -> 0 us
  Pallas kernels: 43.1 us -> 44.8 us
  between operations: 2.33 us -> 0.64 us
    unnamed x4 -> x0, local copies, waits for them, and re-layouts: 5.34 us -> none
    pallas_call x0 -> x1, Pallas kernels: none -> 2.19 us  [step(): pl.pallas_call(hand_out, out_shape=shapes, in_specs=[vmem] * 5, out_specs...]
where the time goes in v3:
time: 45.7 us; the launch traced here: 45.5 us
  Pallas kernels  44.8 us (98%)
  between operations  0.64 us (1%)
    pallas_call x1, Pallas kernels, step(): pl.pallas_call(functools.partial(kernel, n_scen, n_clus, clus_here, quart...  42.7 us
    pallas_call x1, Pallas kernels, step(): pl.pallas_call(hand_out, out_shape=shapes, in_specs=[vmem] * 5, out_specs...  2.19 us

profile of v3, /device:TPU:1, one launch (start us, length us, event | category | flops | bytes accessed | tf_op | source)
XLA Modules:
  0.0 45.5 jit_solution(12764773837192726502)
XLA Ops:
  0.6 42.7 %shard_map.137 = (f32[16,4,192]{2,1,0:T(4,128)}, f32[16,96]{1,0:T(8,128)}, f32[16,96]{1,0:T(8,128)}, f32[8,96]{1,0:T(8,128)}, f32[1,1]{1,0:T(1,128)}) custom-call(bf16[16,1152,128]{2,1,0:T(8,128)(2,1)} %bitcast.9, f32[16,4,192]{2,1,0:T(4,128)} %lin_hbm.1, s32[4,16]{1,0:T(4,128)} %bitcast.10, s32[4,16]{1,0:T(4,128)} %bitcast.11, s32[4]{0:T(128)} %ev_hbm.1, ...), custom_call_target="tpu_custom_call" | custom-call | tf_op jit(solution)/shard_map/pallas_call | solution.py:497
  43.3 2.2 %shard_map.138 = (f32[16,4,192]{2,1,0:T(4,128)}, f32[16,96]{1,0:T(8,128)}, f32[16,96]{1,0:T(8,128)}, f32[8,96]{1,0:T(8,128)}, f32[1,1]{1,0:T(1,128)}) custom-call(f32[16,4,192]{2,1,0:T(4,128)} %get-tuple-element.15.refs_0_, f32[16,96]{1,0:T(8,128)} %get-tuple-element.16.refs_1_, f32[16,96]{1,0:T(8,128)} %get-tuple-element.17.refs_2_, ...), custom_call_target="tpu_custom_call" | custom-call | tf_op jit(solution)/shard_map/pallas_call | solution.py:549

commit v4 on v3

--- a/solution.py
+++ b/solution.py
@@ -26,14 +26,14 @@
     return jnp.broadcast_to(tile[p : p + 1, :], (8, LANES))
 
 
-def eliminate(system, quarter):
-    height = quarter + 8
+def sweep(matrix, first, count, trips):
+    height = matrix.shape[0]
     lane = iota((8, LANES), 1)
     sub = iota((8, LANES), 0)
     lane_all = iota((height, LANES), 1)
 
     def trip(k, matrix):
-        base = 8 * k
+        base = first + 8 * k
         columns = [
             jnp.take_along_axis(matrix, jnp.full((height, LANES), base + q, jnp.int32), axis=1)
             for q in range(8)
@@ -58,9 +58,18 @@
         while len(terms) > 1:
             terms = [terms[i] + terms[i + 1] for i in range(0, len(terms), 2)]
         matrix = jnp.where(taken, 0.0, matrix) - terms[0]
-        return jnp.concatenate([matrix[8:quarter], matrix[:8], matrix[quarter:]], axis=0)
-
-    return lax.fori_loop(0, quarter // 8, trip, system)
+        return jnp.concatenate([matrix[8:count], matrix[:8], matrix[count:]], axis=0)
+
+    return lax.fori_loop(0, trips, trip, matrix)
+
+
+def solve_row(system, side_rows, quarter):
+    half = quarter // 2
+    matrix = jnp.concatenate([system, side_rows], axis=0)
+    matrix = sweep(matrix, 0, quarter, half // 8)
+    matrix = jnp.concatenate([matrix[:half], matrix[quarter:]], axis=0)
+    matrix = sweep(matrix, half, half, half // 8)
+    return matrix[half : half + 1]
 
 
 def kernel(
@@ -287,8 +296,8 @@
         pt_buf[s] = paired
         pushed_rows = jnp.broadcast_to(pushed, (16, 2 * rows)).astype(BF16)
         left = jnp.concatenate([paired, pushed_rows], axis=0)
-        right = jnp.concatenate([left, jnp.zeros((16, 2 * rows), BF16)], axis=0)
-        product = dot_nt(left, right)
+        product = dot_nt(left, paired)
+        product = jnp.concatenate([product, jnp.zeros((quarter + 16, LANES - quarter), F32)], axis=1)
         schur = product[:quarter]
         low = pltpu.roll(schur[half:], LANES - half, 1)
         send_m[s] = jnp.where(below, low, schur[:half]).astype(BF16)
@@ -354,8 +363,7 @@
     system = jnp.where(lane_q < quarter, system, 0.0)
     side = jnp.where(lane1 < quarter, mult - penalty * (vec[0:1] + anchor), 0.0)
     side_rows = jnp.where(sub8 == 0, side, 0.0)
-    solved = eliminate(jnp.concatenate([system, side_rows], axis=0), quarter)
-    prices = solved[quarter : quarter + 1]
+    prices = solve_row(system, side_rows, quarter)
     bid = anchor + (prices - mult) / penalty
     msg[0:1, :] = prices
     msg[1:2, :] = jnp.where(lane1 < quarter, bid, jnp.where(lane1 == quarter, 1.0, 0.0))
@@ -498,7 +506,7 @@
             functools.partial(
                 kernel, n_scen, n_clus, clus_here, quarter, split_at, branch_count
             ),
-            out_shape=shapes,
+            out_shape=tuple(pltpu.VMEM(shape.shape, shape.dtype) for shape in shapes),
             in_specs=[pl.BlockSpec(memory_space=pl.ANY)] * 10,
             out_specs=(vmem,) * 5,
             scratch_shapes=[
@@ -548,7 +556,7 @@
         )
         power, bid, following, mean, gap = pl.pallas_call(
             hand_out, out_shape=shapes, in_specs=[vmem] * 5, out_specs=(vmem,) * 5
-        )(*results)
+        )(*[pltpu.with_memory_space_constraint(result, pltpu.VMEM) for result in results])
         return (power, bid, following, mean, gap.reshape(()))
 
     return jax.shard_map(

time: 45.7 us -> 44.1 us (0.965)
  Pallas kernels: 44.8 us -> 43.4 us
    pallas_call x1, Pallas kernels: 2.19 us -> 1.28 us  [step(): pl.pallas_call(hand_out, out_shape=shapes, in_specs=[vmem] * 5, out_specs...]
    pallas_call x1, Pallas kernels: 42.7 us -> 42.1 us  [step(): pl.pallas_call(functools.partial(kernel, n_scen, n_clus, clus_here, quart...]
where the time goes in v4:
time: 44.1 us; the launch traced here: 44 us
  Pallas kernels  43.4 us (98%)
  between operations  0.64 us (1%)
    pallas_call x1, Pallas kernels, step(): pl.pallas_call(functools.partial(kernel, n_scen, n_clus, clus_here, quart...  42.1 us
    pallas_call x1, Pallas kernels, step(): pl.pallas_call(hand_out, out_shape=shapes, in_specs=[vmem] * 5, out_specs...  1.28 us

profile of v4, /device:TPU:1, one launch (start us, length us, event | category | flops | bytes accessed | tf_op | source)
XLA Modules:
  0.0 44.0 jit_solution(11934709905452628180)
XLA Ops:
  0.6 42.1 %shard_map.137 = (f32[16,4,192]{2,1,0:T(4,128)S(1)}, f32[16,96]{1,0:T(8,128)S(1)}, f32[16,96]{1,0:T(8,128)S(1)}, f32[8,96]{1,0:T(8,128)S(1)}, f32[1,1]{1,0:T(1,128)}) custom-call(bf16[16,1152,128]{2,1,0:T(8,128)(2,1)} %bitcast.9, f32[16,4,192]{2,1,0:T(4,128)} %lin_hbm.1, s32[4,16]{1,0:T(4,128)} %bitcast.10, s32[4,16]{1,0:T(4,128)} %bitcast.11, s32[4]{0:T(128)} %ev_hbm.1, ...), custom_call_target="tpu_custom_call" | custom-call | tf_op jit(solution)/shard_map/pallas_call | solution.py:505
  42.7 1.3 %shard_map.138 = (f32[16,4,192]{2,1,0:T(4,128)}, f32[16,96]{1,0:T(8,128)}, f32[16,96]{1,0:T(8,128)}, f32[8,96]{1,0:T(8,128)}, f32[1,1]{1,0:T(1,128)}) custom-call(f32[16,4,192]{2,1,0:T(4,128)S(1)} %get-tuple-element.15.refs_0_, f32[16,96]{1,0:T(8,128)S(1)} %get-tuple-element.16.refs_1_, f32[16,96]{1,0:T(8,128)S(1)} %get-tuple-element.17.refs_2_, ...), custom_call_target="tpu_custom_call" | custom-call | tf_op jit(solution)/shard_map/pallas_call | solution.py:557

commit v5 on v4

--- a/solution.py
+++ b/solution.py
@@ -369,12 +369,9 @@
     msg[1:2, :] = jnp.where(lane1 < quarter, bid, jnp.where(lane1 == quarter, 1.0, 0.0))
     recv_p[my_slot] = msg[...]
 
-    def send_p(j, carry):
+    for j in sorted(range(1, plane), key=lambda j: abs(2 * j - plane)):
         slot = lax.rem(my_slot + j, plane)
         remote(msg, recv_p.at[my_slot], 3, plane_device(slot)).start()
-        return carry
-
-    lax.fori_loop(1, plane, send_p, 0, unroll=True)
     await_all(recv_p, 3, recv_sem, plane - 1)
 
     def bid_tile(i):
@@ -397,12 +394,9 @@
     )
     recv_s[my_inner] = stat[...]
 
-    def send_s(j, carry):
+    for j in sorted(range(1, inner), key=lambda j: abs(2 * j - inner)):
         slot = lax.rem(my_inner + j, inner)
         remote(stat, recv_s.at[my_inner], 4, line_device(slot)).start()
-        return carry
-
-    lax.fori_loop(1, inner, send_s, 0, unroll=True)
 
     def powers(s, carry):
         price = recv_p[my_base + s, 0:1, :][:, :quarter]
@@ -464,8 +458,14 @@
 
 def hand_out(*refs):
     count = len(refs) // 2
-    for source, target in zip(refs[:count], refs[count:]):
-        target[...] = source[...]
+    sems = refs[-1]
+    copies = [
+        pltpu.make_async_copy(refs[i], refs[count + i], sems.at[i]) for i in range(count)
+    ]
+    for copy in copies:
+        copy.start()
+    for copy in copies:
+        copy.wait()
 
 
 def solution(mesh):
@@ -555,7 +555,11 @@
             branch_prev,
         )
         power, bid, following, mean, gap = pl.pallas_call(
-            hand_out, out_shape=shapes, in_specs=[vmem] * 5, out_specs=(vmem,) * 5
+            hand_out,
+            out_shape=shapes,
+            in_specs=[vmem] * 5,
+            out_specs=(pl.BlockSpec(memory_space=pl.ANY),) * 5,
+            scratch_shapes=[dma((5,))],
         )(*[pltpu.with_memory_space_constraint(result, pltpu.VMEM) for result in results])
         return (power, bid, following, mean, gap.reshape(()))
 

time: 44.1 us -> 43.7 us (level)
  Pallas kernels: 43.4 us -> 42.9 us
    pallas_call x1, Pallas kernels: 42.1 us -> 41.6 us  [step(): pl.pallas_call(functools.partial(kernel, n_scen, n_clus, clus_here, quart...]
where the time goes in v5:
time: 43.7 us; the launch traced here: 43.6 us
  Pallas kernels  42.9 us (98%)
  between operations  0.64 us (1%)
    pallas_call x1, Pallas kernels, step(): pl.pallas_call(functools.partial(kernel, n_scen, n_clus, clus_here, quart...  41.6 us
    pallas_call x1, Pallas kernels, step(): pl.pallas_call(hand_out, out_shape=shapes, in_specs=[vmem] * 5, out_specs...  1.31 us

profile of v5, /device:TPU:1, one launch (start us, length us, event | category | flops | bytes accessed | tf_op | source)
XLA Modules:
  0.0 43.6 jit_solution(11063218913332235836)
XLA Ops:
  0.6 41.6 %shard_map.137 = (f32[16,4,192]{2,1,0:T(4,128)S(1)}, f32[16,96]{1,0:T(8,128)S(1)}, f32[16,96]{1,0:T(8,128)S(1)}, f32[8,96]{1,0:T(8,128)S(1)}, f32[1,1]{1,0:T(1,128)}) custom-call(bf16[16,1152,128]{2,1,0:T(8,128)(2,1)} %bitcast.9, f32[16,4,192]{2,1,0:T(4,128)} %lin_hbm.1, s32[4,16]{1,0:T(4,128)} %bitcast.10, s32[4,16]{1,0:T(4,128)} %bitcast.11, s32[4]{0:T(128)} %ev_hbm.1, ...), custom_call_target="tpu_custom_call" | custom-call | tf_op jit(solution)/shard_map/pallas_call | solution.py:505
  42.2 1.3 %shard_map.138 = (f32[16,4,192]{2,1,0:T(4,128)}, f32[16,96]{1,0:T(8,128)}, f32[16,96]{1,0:T(8,128)}, f32[8,96]{1,0:T(8,128)}, f32[1,1]{1,0:T(1,128)}) custom-call(f32[16,4,192]{2,1,0:T(4,128)S(1)} %get-tuple-element.15.refs_0_, f32[16,96]{1,0:T(8,128)S(1)} %get-tuple-element.16.refs_1_, f32[16,96]{1,0:T(8,128)S(1)} %get-tuple-element.17.refs_2_, ...), custom_call_target="tpu_custom_call" | custom-call | tf_op jit(solution)/shard_map/pallas_call | solution.py:557
